TPU v7x, 32 devices: a whole 2x2x4 slice. The times are simulated.
32 devices in a mesh: groups: 2 (over x), expert: 2 (over core), tensor: 8 (over z, y).
Axes of the slice: x: 2, y: 2, z: 4, core: 2. Of those that a mesh axis runs over, the one named last changes fastest.
Arguments:
- tokens: bfloat16 [2048, 3072], P(('groups', 'expert', 'tensor')), parts along dimension 0, may hold values from -6 to 6
- expert_ids: int32 [2048, 1], P(('groups', 'expert', 'tensor')), parts along dimension 0, may hold values from 0 to 1; in each aligned block of 64 rows (0 to 63, 64 to 127, ...) at most 48 rows name the same one
- gates: float32 [2048], P(('groups', 'expert', 'tensor')), parts along dimension 0, may hold values from 0.2 to 1
- gate_weight: bfloat16 [2, 3072, 16384], P('expert', None, 'tensor'), may hold values from -0.109375 to 0.109375
- up_weight: bfloat16 [2, 3072, 16384], P('expert', None, 'tensor'), may hold values from -0.109375 to 0.109375
- down_weight: bfloat16 [2, 16384, 3072], P('expert', 'tensor'), may hold values from -0.046875 to 0.046875
Outputs:
- routed: bfloat16 [2048, 3072], P(('groups', 'expert', 'tensor')), parts along dimension 0
There are 2 independent parts, one for each index of `groups`. A program takes and returns all parts, laid end to end along the dimension named above; an argument that names none is the same for every part. Nothing has to cross between parts.
Inputs may be any that keep to these rules, and one draw needn't show every extreme that they name: `expert_ids`: among the 64 rows of one device no expert is named more than 48 times; in every draw some device names one expert exactly 48 times.
All inputs are finite; a program needn't handle non-finite values.
Results may differ from a plain program's by a relative error of at most 0.014.
Values may be sent and summed in bfloat16 or wider, within the bound.
A program may use at most 128 MiB of HBM per device.

v0:
```python
import jax
import jax.numpy as jnp
from jax import lax
from jax.sharding import PartitionSpec as P

CAP = 48


def slot_table(expert_ids, experts):
    expert_of = expert_ids[:, 0]
    matches = (expert_of[:, None] == jnp.arange(experts, dtype=jnp.int32)[None, :]).astype(
        jnp.int32
    )
    earlier = jnp.cumsum(matches, axis=0) - matches
    position = jnp.sum(earlier * matches, axis=1)
    column = expert_of * CAP + position
    return (column[:, None] == jnp.arange(experts * CAP, dtype=jnp.int32)[None, :]).astype(
        jnp.bfloat16
    )


def per_device(tokens, expert_ids, gates, gate_weight, up_weight, down_weight):
    width = tokens.shape[1]
    experts = lax.axis_size("expert") * gate_weight.shape[0]
    tensor_size = lax.axis_size("tensor")
    local_table = slot_table(expert_ids, experts)
    group_tokens, group_ids = (
        lax.all_gather(tokens, "tensor", axis=0, tiled=True),
        lax.all_gather(expert_ids, "tensor", axis=0, tiled=True),
    )
    tables = jax.vmap(slot_table, in_axes=(0, None))(group_ids.reshape(tensor_size, -1, 1), experts)
    outgoing = jnp.einsum(
        "trj,trd->tjd",
        tables,
        group_tokens.reshape(tensor_size, -1, width),
        preferred_element_type=jnp.float32,
    )
    outgoing = outgoing.astype(jnp.bfloat16).reshape(tensor_size, experts, CAP, width)
    arrived = lax.all_to_all(outgoing, "expert", split_axis=1, concat_axis=1, tiled=True).reshape(
        tensor_size * experts * CAP, width
    )
    gate_pre = jnp.dot(arrived, gate_weight[0], preferred_element_type=jnp.float32)
    up_pre = jnp.dot(arrived, up_weight[0], preferred_element_type=jnp.float32)
    hidden = (jax.nn.gelu(gate_pre, approximate=True) * up_pre).astype(jnp.bfloat16)
    feature_count = hidden.shape[1]
    ordered = hidden.reshape(tensor_size, experts, CAP, feature_count)
    ordered = jnp.transpose(ordered, (1, 0, 2, 3)).reshape(
        experts * tensor_size * CAP, feature_count
    )
    own_expert = (jnp.arange(experts, dtype=jnp.int32) == lax.axis_index("expert")).astype(
        jnp.float32
    )
    sources = experts * CAP * lax.axis_size(("expert", "tensor")) // (experts * CAP)
    product = jnp.dot(ordered, down_weight[0], preferred_element_type=jnp.float32)
    product = product.reshape(sources, 1, CAP, width) * own_expert[None, :, None, None]
    summed = lax.psum_scatter(
        product.reshape(experts * CAP * lax.axis_size(("expert", "tensor")), width).astype(
            jnp.bfloat16
        ),
        ("expert", "tensor"),
        scatter_dimension=0,
        tiled=True,
    )
    returned = summed.reshape(experts, CAP, width)
    picked = jnp.dot(
        local_table, returned.reshape(experts * CAP, width), preferred_element_type=jnp.float32
    )
    return (picked * gates[:, None]).astype(jnp.bfloat16)


def solution(mesh):
    return jax.shard_map(
        per_device,
        mesh=mesh,
        in_specs=(
            P(("groups", "expert", "tensor"), None),
            P(("groups", "expert", "tensor"), None),
            P(("groups", "expert", "tensor")),
            P("expert", None, "tensor"),
            P("expert", None, "tensor"),
            P("expert", "tensor", None),
        ),
        out_specs=P(("groups", "expert", "tensor"), None),
        check_vma=False,
    )
```

profile of v0, /device:TPU:0, one launch (start us, length us, event | category | flops | bytes accessed | tf_op | source)
XLA Modules:
  0.0 246.8 jit_solution(8364695378265724020)
XLA Ops:
  6.5 0.0 all-gather.2.cloned.1.call-start
  6.5 0.7 all-gather.2.cloned.1.call-update
  7.3 0.0 reduce-scatter.2.cloned.1.call-start
  7.3 1.2 dynamic-slice
  9.2 0.8 bitcast_dynamic-update-slice_fusion
  10.0 13.1 %all-reduce = s32[512]{0:T(512)S(1)} all-reduce(s32[512]{0:T(512)S(1)} %bitcast_dynamic-update-slice_fusion), channel_id=1, replica_groups=mesh['groups'=2,'expert'=2,'tensor'=8] {'tensor'}, use_global_device_ids=true, to_apply=%add | all-reduce | flops 512 | bytes 4096
  23.1 0.1 squeeze_reshape.4
  23.1 0.1 copy.22
  23.2 1.4 fusion.26
  24.6 0.1 copy.23
  24.7 0.1 mul.91
  24.7 0.1 mul.92
  24.8 47.4 %all-gather.2.cloned.1.call-done = bf16[512,3072]{1,0:T(8,128)(2,1)} async-done(((bf16[64,3072]{1,0:T(8,128)(2,1)}), bf16[512,3072]{1,0:T(8,128)(2,1)}) %all-gather.2.cloned.1.call-update) | async-done | bytes 3145744 | tf_op jit(solution)/shard_map/all_gather | solution.py:28
  72.3 3.4 %convolution_convert_fusion = bf16[8,96,3072]{2,1,0:T(8,128)(2,1)S(1)} fusion(bf16[8,64,3072]{2,1,0:T(8,128)(2,1)} %bitcast.40, s32[8,64]{1,0:T(8,128)S(1)} %multiply_add_fusion), kind=kOutput, calls=%fused_computation.18 | convolution fusion | flops 304398336 | bytes 7866368 | tf_op jit(solution)/shard_map/trj,trd->tjd/dot_general | solution.py:32
  75.7 0.0 slice-start
  75.7 0.4 copy.24
  76.1 0.0 slice-start.1
  76.1 7.9 %all_to_all.5 = bf16[8,2,48,3072]{3,2,0,1:T(8,128)(2,1)S(1)} all-to-all(bf16[8,2,48,3072]{3,2,0,1:T(8,128)(2,1)S(1)} %copy.24), channel_id=1, replica_groups=mesh['groups'=2,'expert'=2,'tensor'=8] {'expert'}, dimensions={1} | all-to-all | bytes 9437184 | tf_op jit(solution)/shard_map/all_to_all | solution.py:39
  84.1 0.0 slice-start.2
  84.1 0.4 copy.25
  84.5 0.0 slice-done
  84.5 0.0 slice-done.1
  84.5 1.7 slice-done.2
  86.3 10.0 %fusion.5 = f32[768,2048]{1,0:T(8,128)S(1)} fusion(bf16[768,3072]{1,0:T(8,128)(2,1)S(1)} %bitcast.38, bf16[1,3072,2048]{2,1,0:T(8,128)(2,1)S(1)} %bitcast.46), kind=kOutput, calls=%fused_computation.6 | convolution fusion | flops 9663676416 | bytes 23592960 | tf_op jit(solution)/shard_map/dot_general | solution.py:42
  96.2 14.0 %fusion.15 = bf16[768,2048]{1,0:T(8,128)(2,1)S(1)} fusion(f32[768,2048]{1,0:T(8,128)S(1)} %fusion.5, bf16[768,3072]{1,0:T(8,128)(2,1)S(1)} %bitcast.39, bf16[1,3072,2048]{2,1,0:T(8,128)(2,1)} %param.10), kind=kOutput, calls=%fused_computation.17 | convolution fusion | flops 9679405056 | bytes 26738688 | tf_op jit(solution)/shard_map/dot_general | solution.py:43
  110.3 0.2 copy.26
  110.5 12.8 %fusion.1 = f32[16,48,3072]{2,1,0:T(8,128)S(1)} fusion(bf16[16,48,2048]{2,1,0:T(8,128)(2,1)S(1)} %bitcast.42, bf16[1,2048,3072]{2,1,0:T(8,128)(2,1)} %param.11), kind=kOutput, calls=%fused_computation.2 | convolution fusion | flops 9663676416 | bytes 25165824 | tf_op jit(solution)/shard_map/dot_general | solution.py:54
  123.3 4.5 %fusion = bf16[1536,3072]{1,0:T(8,128)(2,1)} fusion(f32[1536]{0:T(1024)S(1)} %mul.92, f32[16,48,3072]{2,1,0:T(8,128)S(1)} %fusion.1), kind=kLoop, calls=%fused_computation.1 | loop fusion | flops 9437184 | bytes 18880512 | tf_op jit(solution)/shard_map/convert_element_type | solution.py:57
  127.8 0.0 copy-start
  127.8 0.0 copy-start.1
  127.8 0.0 reduce-scatter.2.cloned.1.call-update
  127.8 0.6 copy-done
  128.4 0.1 fusion.23
  128.5 0.1 reduce_window_sum.22
  128.6 0.2 select_reduce_fusion
  128.8 109.0 %reduce-scatter.2.cloned.1.call-done = bf16[96,3072]{1,0:T(8,128)(2,1)} async-done(((bf16[1536,3072]{1,0:T(8,128)(2,1)}), bf16[96,3072]{1,0:T(8,128)(2,1)}) %reduce-scatter.2.cloned.1.call-update) | async-done | bytes 589840 | tf_op jit(solution)/shard_map/reduce_scatter | solution.py:56
  237.8 0.0 copy-done.1
  237.8 2.1 fusion.18
  (5 shorter events, 0.0 us)
Async XLA Ops:
  6.5 65.7 %all-gather.2.cloned.1.call-start = ((), (), s32[]{:S(2)}) async-start(), calls=%async_computation.2 | async-start | bytes 3538944 | tf_op jit(solution)/shard_map/all_gather | solution.py:28
  7.3 230.6 %reduce-scatter.2.cloned.1.call-start = ((), (), s32[]{:S(2)}) async-start(), calls=%async_computation.3 | async-start | bytes 10027008 | tf_op jit(solution)/shard_map/reduce_scatter | solution.py:56
  75.7 8.8 %slice-start = ((s8[12582912]{0:T(1024)(128)(4,1)}), s8[4194304]{0:T(1024)(128)(4,1)S(1)}, s32[]{:S(2)}) async-start(s8[12582912]{0:T(1024)(128)(4,1)} %bitcast.45), calls=%async_computation.4 | async-start | bytes 8388608
  76.1 8.4 %slice-start.1 = ((s8[12582912]{0:T(1024)(128)(4,1)}), s8[4194304]{0:T(1024)(128)(4,1)S(1)}, s32[]{:S(2)}) async-start(s8[12582912]{0:T(1024)(128)(4,1)} %bitcast.45), calls=%async_computation.5 | async-start | bytes 8388608
  84.1 2.2 slice-start.2
  127.8 0.7 copy-start
  127.8 110.1 %copy-start.1 = (f32[64]{0:T(128)S(1)}, f32[64]{0:T(128)}, u32[]{:S(2)}) copy-start(f32[64]{0:T(128)} %param.8) | copy-start | bytes 772
Sparse Core Ops, SparseCore 0:
  9.5 62.7 all-gather.1
  127.9 109.8 reduce-scatter.1
where the time goes:
time: 247 us
  waiting for transfers between devices  157 us (64%)
  matrix products  42.3 us (17%)
  blocking collectives  21 us (9%)
  between operations  14.2 us (6%)
  other arithmetic  6.21 us (3%)
  local copies, waits for them, and re-layouts  5.85 us (2%)
    reduce_scatter x1, waiting for transfers between devices, per_device(): lax.psum_scatter(product.reshape(experts * CAP * lax.axis_size(('expert',...  109 us
    all_gather x1, waiting for transfers between devices, per_device(): lax.all_gather(tokens, 'tensor', axis=0, tiled=True)  47.4 us
    dot_general x1, matrix products, per_device(): up_pre = jnp.dot(arrived, up_weight[0], preferred_element_type=jnp.float32)  14 us
    unnamed x1, blocking collectives  13.1 us
    dot_general x1, matrix products, per_device(): jnp.dot(ordered, down_weight[0], preferred_element_type=jnp.float32)  12.8 us
    dot_general x1, matrix products, per_device(): jnp.dot(arrived, gate_weight[0], preferred_element_type=jnp.float32)  9.97 us
    all_to_all x1, blocking collectives, per_device(): lax.all_to_all(outgoing, 'expert', split_axis=1, concat_axis=1, tiled=True)  7.92 us
  transfers between devices with their start and end apart: 2, of which 2 were waited for; matrix products, arithmetic and copies ran while one was open for 2% of the time, Pallas kernels for 0%

commit v1 on v0

v1 whole, which is shorter than its diff:
```python
import jax
import jax.numpy as jnp
from jax import lax
from jax.sharding import PartitionSpec as P

CAP = 48
IN_CHUNKS = 1
OUT_CHUNKS = 2


def slot_table(expert_ids, experts):
    expert_of = expert_ids[:, 0]
    matches = (expert_of[:, None] == jnp.arange(experts, dtype=jnp.int32)[None, :]).astype(
        jnp.int32
    )
    earlier = jnp.cumsum(matches, axis=0) - matches
    position = jnp.sum(earlier * matches, axis=1)
    column = expert_of * CAP + position
    return (column[:, None] == jnp.arange(experts * CAP, dtype=jnp.int32)[None, :]).astype(
        jnp.bfloat16
    )


def per_device(tokens, expert_ids, gates, gate_weight, up_weight, down_weight):
    rows, width = tokens.shape
    experts = lax.axis_size("expert") * gate_weight.shape[0]
    tensor_size = lax.axis_size("tensor")
    group_ids = lax.all_gather(expert_ids, "tensor", axis=0, tiled=True)
    tables = jax.vmap(slot_table, in_axes=(0, None))(group_ids.reshape(tensor_size, rows, 1), experts)

    gate_pre, up_pre = None, None
    step = width // IN_CHUNKS
    for chunk in range(IN_CHUNKS):
        cut = slice(chunk * step, (chunk + 1) * step)
        gathered = lax.all_gather(tokens[:, cut], "tensor", axis=0)
        outgoing = jnp.einsum("trj,trd->tjd", tables, gathered, preferred_element_type=jnp.float32)
        outgoing = outgoing.astype(jnp.bfloat16).reshape(tensor_size, experts, CAP, step)
        arrived = lax.all_to_all(
            outgoing, "expert", split_axis=1, concat_axis=1, tiled=True
        ).reshape(tensor_size * experts * CAP, step)
        gate_part = jnp.dot(arrived, gate_weight[0, cut], preferred_element_type=jnp.float32)
        up_part = jnp.dot(arrived, up_weight[0, cut], preferred_element_type=jnp.float32)
        gate_pre = gate_part if gate_pre is None else gate_pre + gate_part
        up_pre = up_part if up_pre is None else up_pre + up_part
    hidden = (jax.nn.gelu(gate_pre, approximate=True) * up_pre).astype(jnp.bfloat16)

    step = width // OUT_CHUNKS
    pieces = []
    for chunk in range(OUT_CHUNKS):
        cut = slice(chunk * step, (chunk + 1) * step)
        product = jnp.dot(hidden, down_weight[0, :, cut], preferred_element_type=jnp.float32)
        product = product.astype(jnp.bfloat16).reshape(tensor_size, experts, CAP, step)
        returned = lax.all_to_all(
            product, "expert", split_axis=1, concat_axis=1, tiled=True
        ).reshape(tensor_size, experts * CAP, step)
        placed = jnp.einsum("trj,tjd->trd", tables, returned, preferred_element_type=jnp.float32)
        placed = placed.astype(jnp.bfloat16).reshape(tensor_size * rows, step)
        summed = lax.psum_scatter(placed, "tensor", scatter_dimension=0, tiled=True)
        pieces.append((summed.astype(jnp.float32) * gates[:, None]).astype(jnp.bfloat16))
    return jnp.concatenate(pieces, axis=1) if len(pieces) > 1 else pieces[0]


def solution(mesh):
    return jax.shard_map(
        per_device,
        mesh=mesh,
        in_specs=(
            P(("groups", "expert", "tensor"), None),
            P(("groups", "expert", "tensor"), None),
            P(("groups", "expert", "tensor")),
            P("expert", None, "tensor"),
            P("expert", None, "tensor"),
            P("expert", "tensor", None),
        ),
        out_specs=P(("groups", "expert", "tensor"), None),
        check_vma=False,
    )
```

time: 247 us -> 268 us (1.085)
  blocking collectives: 21 us -> 32.3 us
  waiting for transfers between devices: 157 us -> 165 us
  matrix products: 42.3 us -> 47.3 us
  other arithmetic: 6.21 us -> 3.31 us
    all_to_all x0 -> x2, blocking collectives: none -> 11.3 us  [per_device(): lax.all_to_all(product, 'expert', split_axis=1, concat_axis=1, tiled=True)]
    reduce_scatter x1 -> x2, waiting for transfers between devices: 109 us -> 116 us  [per_device(): summed = lax.psum_scatter(placed, 'tensor', scatter_dimension=0, tiled=True)]
    dot_general x5 -> x7, matrix products: 42.3 us -> 47.3 us  [the longest x2 16.4 us: per_device(): jnp.dot(hidden, down_weight[0, :, cut], preferred_element_type=jnp.float32)]
    convert_element_type x3 -> x1, other arithmetic: 4.55 us -> 1.15 us  [per_device(): (summed.astype(jnp.float32) * gates[:, None]).astype(jnp.bfloat16)]
  transfers between devices with their start and end apart: 2 -> 3, of which waited for: 2 -> 3; matrix products, arithmetic and copies ran while one was open for 2% -> 5% of each run, Pallas kernels for 0% -> 0%
where the time goes in v1:
time: 268 us; the launch traced here: 267 us
  waiting for transfers between devices  165 us (62%)
  matrix products  47.3 us (18%)
  blocking collectives  32.3 us (12%)
  between operations  13.9 us (5%)
  local copies, waits for them, and re-layouts  5.52 us (2%)
  other arithmetic  3.31 us (1%)
    reduce_scatter x2, waiting for transfers between devices, per_device(): summed = lax.psum_scatter(placed, 'tensor', scatter_dimension=0, tiled=True)  116 us
    all_gather x1, waiting for transfers between devices, per_device(): gathered = lax.all_gather(tokens[:, cut], 'tensor', axis=0)  47.6 us
    dot_general x2, matrix products, per_device(): jnp.dot(hidden, down_weight[0, :, cut], preferred_element_type=jnp.float32)  16.4 us
    dot_general x1, matrix products, per_device(): jnp.dot(arrived, up_weight[0, cut], preferred_element_type=jnp.float32)  14 us
    unnamed x1, blocking collectives  13.1 us
    all_to_all x2, blocking collectives, per_device(): lax.all_to_all(product, 'expert', split_axis=1, concat_axis=1, tiled=True)  11.3 us
    dot_general x1, matrix products, per_device(): jnp.dot(arrived, gate_weight[0, cut], preferred_element_type=jnp.float32)  9.97 us
    all_to_all x1, blocking collectives, per_device(): lax.all_to_all(outgoing, 'expert', split_axis=1, concat_axis=1, tiled=True)  7.92 us
  transfers between devices with their start and end apart: 3, of which 3 were waited for; matrix products, arithmetic and copies ran while one was open for 5% of the time, Pallas kernels for 0%

profile of v1, /device:TPU:0, one launch (start us, length us, event | category | flops | bytes accessed | tf_op | source)
XLA Modules:
  0.0 267.2 jit_solution(1103878211246702654)
XLA Ops:
  6.5 0.0 all-gather.3.cloned.1.call-start
  6.5 0.7 all-gather.3.cloned.1.call-update
  7.3 0.0 reduce-scatter.5.cloned.1.call-start
  7.3 1.2 dynamic-slice
  9.2 0.8 bitcast_dynamic-update-slice_fusion
  10.0 13.1 %all-reduce = s32[512]{0:T(512)S(1)} all-reduce(s32[512]{0:T(512)S(1)} %bitcast_dynamic-update-slice_fusion), channel_id=1, replica_groups=mesh['groups'=2,'expert'=2,'tensor'=8] {'tensor'}, use_global_device_ids=true, to_apply=%add | all-reduce | flops 512 | bytes 4096
  23.1 0.1 squeeze_reshape.4
  23.1 0.1 copy.26
  23.2 1.4 fusion.33
  24.6 0.1 copy.27
  24.7 47.6 %all-gather.3.cloned.1.call-done = bf16[512,3072]{1,0:T(8,128)(2,1)} async-done(((bf16[64,3072]{1,0:T(8,128)(2,1)}), bf16[512,3072]{1,0:T(8,128)(2,1)}) %all-gather.3.cloned.1.call-update) | async-done | bytes 3145744 | tf_op jit(solution)/shard_map/all_gather | solution.py:35
  72.3 3.4 %convolution_convert_fusion = bf16[8,96,3072]{2,1,0:T(8,128)(2,1)S(1)} fusion(bf16[8,64,3072]{2,1,0:T(8,128)(2,1)} %bitcast.44, s32[8,64]{1,0:T(8,128)S(1)} %multiply_add_fusion), kind=kOutput, calls=%fused_computation.20 | convolution fusion | flops 304398336 | bytes 7866368 | tf_op jit(solution)/shard_map/trj,trd->tjd/dot_general | solution.py:36
  75.7 0.0 slice-start
  75.7 0.4 copy.28
  76.1 0.0 slice-start.1
  76.1 7.9 %all_to_all.15 = bf16[8,2,48,3072]{3,2,0,1:T(8,128)(2,1)S(1)} all-to-all(bf16[8,2,48,3072]{3,2,0,1:T(8,128)(2,1)S(1)} %copy.28), channel_id=1, replica_groups=mesh['groups'=2,'expert'=2,'tensor'=8] {'expert'}, dimensions={1} | all-to-all | bytes 9437184 | tf_op jit(solution)/shard_map/all_to_all | solution.py:38
  84.1 0.0 slice-start.2
  84.1 0.4 copy.29
  84.5 0.0 slice-done
  84.5 0.0 slice-done.1
  84.5 1.7 slice-done.2
  86.2 10.0 %fusion.2 = f32[768,2048]{1,0:T(8,128)S(1)} fusion(bf16[768,3072]{1,0:T(8,128)(2,1)S(1)} %bitcast.42, bf16[1,3072,2048]{2,1,0:T(8,128)(2,1)S(1)} %bitcast.48), kind=kOutput, calls=%fused_computation.2 | convolution fusion | flops 9663676416 | bytes 23592960 | tf_op jit(solution)/shard_map/dot_general | solution.py:41
  96.2 14.0 %fusion.12 = bf16[768,2048]{1,0:T(8,128)(2,1)S(1)} fusion(f32[768,2048]{1,0:T(8,128)S(1)} %fusion.2, bf16[768,3072]{1,0:T(8,128)(2,1)S(1)} %bitcast.43, bf16[1,3072,2048]{2,1,0:T(8,128)(2,1)} %param.10), kind=kOutput, calls=%fused_computation.13 | convolution fusion | flops 9679405056 | bytes 26738688 | tf_op jit(solution)/shard_map/dot_general | solution.py:42
  110.3 8.3 %fusion.24 = bf16[768,1536]{1,0:T(8,128)(2,1)S(1)} fusion(bf16[768,2048]{1,0:T(8,128)(2,1)S(1)} %fusion.12, bf16[1,2048,3072]{2,1,0:T(8,128)(2,1)} %param.11), kind=kOutput, calls=%fused_computation.22 | convolution fusion | flops 4833017856 | bytes 11796480 | tf_op jit(solution)/shard_map/dot_general | solution.py:51
  118.6 0.2 copy.32
  118.7 5.6 %all_to_all.16 = bf16[8,2,48,1536]{3,2,0,1:T(8,128)(2,1)S(1)} all-to-all(bf16[8,2,48,1536]{3,2,0,1:T(8,128)(2,1)S(1)} %copy.32), channel_id=1, replica_groups=mesh['groups'=2,'expert'=2,'tensor'=8] {'expert'}, dimensions={1} | all-to-all | bytes 4718592 | tf_op jit(solution)/shard_map/all_to_all | solution.py:53
  124.4 0.2 copy.33
  124.5 1.8 convolution_convert_fusion.1
  126.3 0.0 reduce-scatter.5.cloned.1.call-update
  126.4 0.0 reduce-scatter.3.cloned.1.call-start
  126.4 8.1 %fusion.21 = bf16[768,1536]{1,0:T(8,128)(2,1)S(1)} fusion(bf16[768,2048]{1,0:T(8,128)(2,1)S(1)} %fusion.12, bf16[1,2048,3072]{2,1,0:T(8,128)(2,1)} %param.11), kind=kOutput, calls=%fused_computation.21 | convolution fusion | flops 4833017856 | bytes 11796480 | tf_op jit(solution)/shard_map/dot_general | solution.py:51
  134.5 0.2 copy.30
  134.7 5.6 %all_to_all.17 = bf16[8,2,48,1536]{3,2,0,1:T(8,128)(2,1)S(1)} all-to-all(bf16[8,2,48,1536]{3,2,0,1:T(8,128)(2,1)S(1)} %copy.30), channel_id=1, replica_groups=mesh['groups'=2,'expert'=2,'tensor'=8] {'expert'}, dimensions={1} | all-to-all | bytes 4718592 | tf_op jit(solution)/shard_map/all_to_all | solution.py:53
  140.3 0.0 copy-start
  140.3 0.2 copy.31
  140.5 1.8 convolution_convert_fusion.2
  142.3 0.0 reduce-scatter.3.cloned.1.call-update
  142.3 48.5 %reduce-scatter.5.cloned.1.call-done = bf16[64,1536]{1,0:T(8,128)(2,1)} async-done(((bf16[512,1536]{1,0:T(8,128)(2,1)}), bf16[64,1536]{1,0:T(8,128)(2,1)}) %reduce-scatter.5.cloned.1.call-update) | async-done | bytes 196624 | tf_op jit(solution)/shard_map/reduce_scatter | solution.py:58
  190.8 67.9 %reduce-scatter.3.cloned.1.call-done = bf16[64,1536]{1,0:T(8,128)(2,1)} async-done(((bf16[512,1536]{1,0:T(8,128)(2,1)}), bf16[64,1536]{1,0:T(8,128)(2,1)}) %reduce-scatter.3.cloned.1.call-update) | async-done | bytes 196624 | tf_op jit(solution)/shard_map/reduce_scatter | solution.py:58
  258.7 0.0 copy-done
  258.7 1.2 multiply_convert_fusion.1
  259.9 0.8 pad_maximum_fusion
  (3 shorter events, 0.0 us)
Async XLA Ops:
  6.5 65.8 %all-gather.3.cloned.1.call-start = ((), (), s32[]{:S(2)}) async-start(), calls=%async_computation.7 | async-start | bytes 3538944 | tf_op jit(solution)/shard_map/all_gather | solution.py:35
  7.3 183.5 %reduce-scatter.5.cloned.1.call-start = ((), (), s32[]{:S(2)}) async-start(), calls=%async_computation.6 | async-start | bytes 1769472 | tf_op jit(solution)/shard_map/reduce_scatter | solution.py:58
  75.7 8.8 %slice-start = ((s8[12582912]{0:T(1024)(128)(4,1)}), s8[4194304]{0:T(1024)(128)(4,1)S(1)}, s32[]{:S(2)}) async-start(s8[12582912]{0:T(1024)(128)(4,1)} %bitcast.47), calls=%async_computation.8 | async-start | bytes 8388608
  76.1 8.4 %slice-start.1 = ((s8[12582912]{0:T(1024)(128)(4,1)}), s8[4194304]{0:T(1024)(128)(4,1)S(1)}, s32[]{:S(2)}) async-start(s8[12582912]{0:T(1024)(128)(4,1)} %bitcast.47), calls=%async_computation.9 | async-start | bytes 8388608
  84.1 2.2 slice-start.2
  126.4 132.3 %reduce-scatter.3.cloned.1.call-start = ((), (), s32[]{:S(2)}) async-start(), calls=%async_computation.5 | async-start | bytes 1769472 | tf_op jit(solution)/shard_map/reduce_scatter | solution.py:58
  140.3 118.4 %copy-start = (f32[64]{0:T(128)S(1)}, f32[64]{0:T(128)}, u32[]{:S(2)}) copy-start(f32[64]{0:T(128)} %param.8) | copy-start | bytes 772
Sparse Core Ops, SparseCore 0:
  9.5 62.7 all-gather.2
  126.5 64.2 reduce-scatter.4
  194.2 64.4 reduce-scatter.2

commit v2 on v1

v2 whole, which is shorter than its diff:
```python
import functools

import jax
import jax.numpy as jnp
from jax import lax
from jax.experimental import pallas as pl
from jax.experimental.pallas import tpu as pltpu
from jax.sharding import PartitionSpec as P

CAP = 48
LANES = 128
STREAMS = 4


def place_of(zigzag, size, index):
    if not zigzag:
        return index
    odd = index % 2
    return (1 - odd) * (index // 2) + odd * (size - 1 - index // 2)


def index_of(zigzag, size, place):
    place = (place + 2 * size) % size
    if not zigzag:
        return place
    back = place // (size // 2)
    return (1 - back) * (2 * place) + back * (2 * (size - 1 - place) + 1)


def greet(zigzag, size, place):
    barrier = pltpu.get_barrier_semaphore()
    for way in (1, -1):
        pl.semaphore_signal(
            barrier,
            inc=1,
            device_id={"tensor": index_of(zigzag, size, place + way)},
            device_id_type=pl.DeviceIdType.MESH,
        )
    pl.semaphore_wait(barrier, 2)


def send(zigzag, size, place, way, source, target, send_sem, recv_sem):
    return pltpu.make_async_remote_copy(
        src_ref=source,
        dst_ref=target,
        send_sem=send_sem,
        recv_sem=recv_sem,
        device_id={"tensor": index_of(zigzag, size, place + way)},
        device_id_type=pl.DeviceIdType.MESH,
    )


def gather_kernel(zigzag, size, tokens, column, all_tokens, all_columns, send_sem, recv_sem):
    me = lax.axis_index("tensor")
    place = place_of(zigzag, size, me)
    greet(zigzag, size, place)
    part = tokens.shape[1] // STREAMS
    streams = [(column, all_columns, slice(0, LANES), 1)]
    for number in range(STREAMS):
        cut = slice(number * part, (number + 1) * part)
        streams.append((tokens, all_tokens, cut, 1 - 2 * (number % 2)))
    copies = {}
    for step in range(size - 1):
        for number, (mine, whole, cut, way) in enumerate(streams):
            owner = index_of(zigzag, size, place - way * step)
            target = whole.at[owner, :, cut]
            source = mine.at[:, cut]
            if step:
                copies[step - 1, number].wait_recv()
                source = target
            copies[step, number] = send(
                zigzag, size, place, way, source, target,
                send_sem.at[step, number], recv_sem.at[step, number],
            )
            copies[step, number].start()
        if step == 0:
            all_tokens[me] = tokens[...]
            all_columns[me] = column[...]
    for number in range(len(streams)):
        copies[size - 2, number].wait_recv()
    for copy in copies.values():
        copy.wait_send()


def reduce_kernel(zigzag, size, terms, out, held, send_sem, recv_sem):
    me = lax.axis_index("tensor")
    place = place_of(zigzag, size, me)
    greet(zigzag, size, place)
    part = terms.shape[2] // STREAMS
    copies = {}
    for step in range(size):
        for number in range(STREAMS):
            cut = slice(number * part, (number + 1) * part)
            way = 1 - 2 * (number % 2)
            owner = index_of(zigzag, size, place - way * (1 + step))
            source = terms.at[owner, :, cut]
            if step:
                copies[step - 1, number].wait_recv()
                total = held[step - 1, number].astype(jnp.float32) + terms[
                    owner, :, cut
                ].astype(jnp.float32)
                if step == size - 1:
                    out[:, cut] = total.astype(out.dtype)
                    continue
                held[step - 1, number] = total.astype(held.dtype)
                source = held.at[step - 1, number]
            copies[step, number] = send(
                zigzag, size, place, way, source, held.at[step, number],
                send_sem.at[step, number], recv_sem.at[step, number],
            )
            copies[step, number].start()
    for copy in copies.values():
        copy.wait_send()


def ring_gather(zigzag, tokens, column):
    size = lax.axis_size("tensor")
    vmem = pl.BlockSpec(memory_space=pltpu.VMEM)
    sems = pltpu.SemaphoreType.DMA((size - 1, STREAMS + 1))
    return pl.pallas_call(
        functools.partial(gather_kernel, zigzag, size),
        out_shape=(
            jax.ShapeDtypeStruct((size, *tokens.shape), tokens.dtype),
            jax.ShapeDtypeStruct((size, *column.shape), column.dtype),
        ),
        in_specs=[vmem, vmem],
        out_specs=(vmem, vmem),
        scratch_shapes=[sems, sems],
        compiler_params=pltpu.CompilerParams(collective_id=0, has_side_effects=True),
        name="ring_gather",
    )(tokens, column)


def ring_reduce(zigzag, terms):
    size, rows, width = terms.shape
    vmem = pl.BlockSpec(memory_space=pltpu.VMEM)
    sems = pltpu.SemaphoreType.DMA((size - 1, STREAMS))
    return pl.pallas_call(
        functools.partial(reduce_kernel, zigzag, size),
        out_shape=jax.ShapeDtypeStruct((rows, width), terms.dtype),
        in_specs=[vmem],
        out_specs=vmem,
        scratch_shapes=[
            pltpu.VMEM((size - 1, STREAMS, rows, width // STREAMS), terms.dtype),
            sems,
            sems,
        ],
        compiler_params=pltpu.CompilerParams(collective_id=1, has_side_effects=True),
        name="ring_reduce",
    )(terms)


def slot_of(expert_ids, experts):
    expert_of = expert_ids[:, 0]
    matches = (expert_of[:, None] == jnp.arange(experts, dtype=jnp.int32)[None, :]).astype(
        jnp.int32
    )
    earlier = jnp.cumsum(matches, axis=0) - matches
    position = jnp.sum(earlier * matches, axis=1)
    return expert_of * CAP + position


def per_device(zigzag, tokens, expert_ids, gates, gate_weight, up_weight, down_weight):
    rows, width = tokens.shape
    experts = lax.axis_size("expert") * gate_weight.shape[0]
    size = lax.axis_size("tensor")
    column = jnp.broadcast_to(
        slot_of(expert_ids, experts).astype(jnp.bfloat16)[:, None], (rows, LANES)
    )
    gathered, columns = ring_gather(zigzag, tokens, column)
    slots = jnp.arange(experts * CAP, dtype=jnp.float32)
    tables = (columns[:, :, :1].astype(jnp.float32) == slots).astype(jnp.bfloat16)

    outgoing = jnp.einsum("trj,trd->tjd", tables, gathered, preferred_element_type=jnp.float32)
    outgoing = outgoing.astype(jnp.bfloat16).reshape(size, experts, CAP, width)
    arrived = lax.all_to_all(
        outgoing, "expert", split_axis=1, concat_axis=1, tiled=True
    ).reshape(size * experts * CAP, width)
    gate_pre = jnp.dot(arrived, gate_weight[0], preferred_element_type=jnp.float32)
    up_pre = jnp.dot(arrived, up_weight[0], preferred_element_type=jnp.float32)
    hidden = (jax.nn.gelu(gate_pre, approximate=True) * up_pre).astype(jnp.bfloat16)

    product = jnp.dot(hidden, down_weight[0], preferred_element_type=jnp.float32)
    product = product.astype(jnp.bfloat16).reshape(size, experts, CAP, width)
    returned = lax.all_to_all(
        product, "expert", split_axis=1, concat_axis=1, tiled=True
    ).reshape(size, experts * CAP, width)
    placed = jnp.einsum("trj,tjd->trd", tables, returned, preferred_element_type=jnp.float32)
    summed = ring_reduce(zigzag, placed.astype(jnp.bfloat16))
    return (summed.astype(jnp.float32) * gates[:, None]).astype(jnp.bfloat16)


def folds(mesh):
    names = mesh.axis_names
    line = mesh.devices.transpose(
        [names.index("groups"), names.index("expert"), names.index("tensor")]
    )[0, 0]
    coords = [getattr(device, "coords", None) for device in line[:2]]
    return line.size % 2 == 0 and (coords[0] is None or coords[0][2] == coords[1][2])


def solution(mesh):
    return jax.shard_map(
        functools.partial(per_device, folds(mesh)),
        mesh=mesh,
        in_specs=(
            P(("groups", "expert", "tensor"), None),
            P(("groups", "expert", "tensor"), None),
            P(("groups", "expert", "tensor")),
            P("expert", None, "tensor"),
            P("expert", None, "tensor"),
            P("expert", "tensor", None),
        ),
        out_specs=P(("groups", "expert", "tensor"), None),
        check_vma=False,
    )
```

time: 268 us -> 158 us (0.59)
  waiting for transfers between devices: 165 us -> 0 us
  Pallas kernels: 0 us -> 78.8 us
  blocking collectives: 32.3 us -> 15.4 us
  between operations: 13.9 us -> 0.13 us
  local copies, waits for them, and re-layouts: 5.52 us -> 8.51 us
    reduce_scatter x2 -> x0, waiting for transfers between devices: 116 us -> none  [per_device(): summed = lax.psum_scatter(placed, 'tensor', scatter_dimension=0, tiled=True)]
    pallas_call x0 -> x2, Pallas kernels: none -> 78.8 us  [the longest x1 41.3 us: ring_gather(): pl.pallas_call(functools.partial(gather_kernel, zigzag, size), out_shape=...]
    all_gather x1 -> x0, waiting for transfers between devices: 47.6 us -> none  [per_device(): gathered = lax.all_gather(tokens[:, cut], 'tensor', axis=0)]
    unnamed x1 -> x0, blocking collectives: 13.1 us -> none
    all_to_all x2 -> x1, blocking collectives: 11.3 us -> 7.52 us  [per_device(): lax.all_to_all(product, 'expert', split_axis=1, concat_axis=1, tiled=True)]
    dot_general x4 -> x2, matrix products: 40.4 us -> 43.7 us  [the longest x1 31.8 us: per_device(): jnp.dot(hidden, down_weight[0], preferred_element_type=jnp.float32)]
  transfers between devices with their start and end apart: 3 -> 0, of which waited for: 3 -> 0; matrix products, arithmetic and copies ran while one was open for 5% -> 0% of each run, Pallas kernels for 0% -> 0%
where the time goes in v2:
time: 158 us
  Pallas kernels  78.8 us (50%)
  matrix products  49.7 us (31%)
  blocking collectives  15.4 us (10%)
  local copies, waits for them, and re-layouts  8.51 us (5%)
  other arithmetic  5.25 us (3%)
    pallas_call x1, Pallas kernels, ring_gather(): pl.pallas_call(functools.partial(gather_kernel, zigzag, size), out_shape=...  41.3 us
    pallas_call x1, Pallas kernels, ring_reduce(): pl.pallas_call(functools.partial(reduce_kernel, zigzag, size), out_shape=...  37.5 us
    dot_general x1, matrix products, per_device(): jnp.dot(hidden, down_weight[0], preferred_element_type=jnp.float32)  31.8 us
    dot_general x1, matrix products, per_device(): jnp.dot(arrived, gate_weight[0], preferred_element_type=jnp.float32)  11.8 us
    all_to_all x1, blocking collectives, per_device(): lax.all_to_all(outgoing, 'expert', split_axis=1, concat_axis=1, tiled=True)  7.92 us
    all_to_all x1, blocking collectives, per_device(): lax.all_to_all(product, 'expert', split_axis=1, concat_axis=1, tiled=True)  7.52 us
    unnamed x14, local copies, waits for them, and re-layouts  3.71 us
    dot_general x1, matrix products, per_device(): jnp.einsum('trj,trd->tjd', tables, gathered, preferred_element_type=jnp.f...  3.39 us

profile of v2, /device:TPU:0, one launch (start us, length us, event | category | flops | bytes accessed | tf_op | source)
XLA Modules:
  0.0 157.9 jit_solution(9598790192341857432)
XLA Ops:
  0.0 0.7 fusion.28
  0.7 0.1 reduce_window_sum.11
  0.8 0.8 select_reduce_fusion
  1.7 0.7 fusion.30
  2.3 0.7 broadcast_in_dim.5.column
  3.0 41.3 %ring_gather.1 = (bf16[8,64,3072]{2,1,0:T(8,128)(2,1)}, bf16[8,64,128]{2,1,0:T(8,128)(2,1)}) custom-call(bf16[64,3072]{1,0:T(8,128)(2,1)} %tokens.1, bf16[64,128]{1,0:T(8,128)(2,1)} %broadcast_in_dim.5.column), custom_call_target="tpu_custom_call" | custom-call | tf_op jit(solution)/shard_map/ring_gather/pallas_call | solution.py:120
  44.3 1.0 convert_reduce_fusion
  45.4 0.0 copy-start.1
  45.4 3.4 %convolution_convert_fusion = bf16[8,96,3072]{2,1,0:T(8,128)(2,1)S(1)} fusion(bf16[8,64,3072]{2,1,0:T(8,128)(2,1)} %get-tuple-element.8, f32[8,64]{1,0:T(8,128)S(1)} %convert_reduce_fusion), kind=kOutput, calls=%fused_computation.17 | convolution fusion | flops 304398336 | bytes 7866368 | tf_op jit(solution)/shard_map/trj,trd->tjd/dot_general | solution.py:174
  48.8 0.0 copy-done.1
  48.8 0.0 slice-start
  48.8 0.4 copy.10
  49.2 0.0 slice-start.1
  49.2 7.9 %all_to_all.10 = bf16[8,2,48,3072]{3,2,0,1:T(8,128)(2,1)S(1)} all-to-all(bf16[8,2,48,3072]{3,2,0,1:T(8,128)(2,1)S(1)} %copy.10), channel_id=1, replica_groups=mesh['groups'=2,'expert'=2,'tensor'=8] {'expert'}, dimensions={1} | all-to-all | bytes 9437184 | tf_op jit(solution)/shard_map/all_to_all | solution.py:176
  57.2 0.0 slice-start.2
  57.2 0.4 copy.11
  57.6 0.0 copy-start
  57.6 2.4 %copy-done = bf16[8,2,48,3072]{3,2,1,0:T(8,128)(2,1)} copy-done((bf16[8,2,48,3072]{3,2,1,0:T(8,128)(2,1)}, bf16[8,2,48,3072]{3,2,1,0:T(8,128)(2,1)S(1)}, u32[]{:S(2)}) %copy-start) | copy-done | bytes 4718616
  60.0 0.0 slice-done
  60.0 0.0 slice-done.1
  60.0 1.0 slice-done.2
  61.1 11.8 %fusion.4 = f32[768,2048]{1,0:T(8,128)} fusion(bf16[768,3072]{1,0:T(8,128)(2,1)S(1)} %bitcast.34, bf16[1,3072,2048]{2,1,0:T(8,128)(2,1)S(1)} %bitcast.40), kind=kOutput, calls=%fused_computation.4 | convolution fusion | flops 9663676416 | bytes 23592960 | tf_op jit(solution)/shard_map/dot_general | solution.py:179
  72.9 31.8 %fusion.15 = bf16[768,3072]{1,0:T(8,128)(2,1)} fusion(bf16[1,2048,3072]{2,1,0:T(8,128)(2,1)} %param.11, f32[768,2048]{1,0:T(8,128)} %fusion.4, bf16[768,3072]{1,0:T(8,128)(2,1)} %bitcast.35, bf16[1,3072,2048]{2,1,0:T(8,128)(2,1)} %param.10), kind=kOutput, calls=%fused_computation.16 | convolution fusion | flops 19345440768 | bytes 40894464 | tf_op jit(solution)/shard_map/dot_general | solution.py:183
  104.7 2.8 %copy.12 = bf16[8,2,48,3072]{3,2,0,1:T(8,128)(2,1)S(1)} copy(bf16[8,2,48,3072]{3,2,1,0:T(8,128)(2,1)} %bitcast.36) | data formatting | bytes 9437184 | tf_op jit(solution)/shard_map/reshape | solution.py:184
  107.6 7.5 %all_to_all.11 = bf16[8,2,48,3072]{3,2,0,1:T(8,128)(2,1)S(1)} all-to-all(bf16[8,2,48,3072]{3,2,0,1:T(8,128)(2,1)S(1)} %copy.12), channel_id=1, replica_groups=mesh['groups'=2,'expert'=2,'tensor'=8] {'expert'}, dimensions={1} | all-to-all | bytes 9437184 | tf_op jit(solution)/shard_map/all_to_all | solution.py:185
  115.1 0.0 copy-start.2
  115.1 0.4 copy.13
  115.5 0.0 copy-start.3
  115.5 0.2 copy-done.2
  115.8 2.7 %convolution_convert_fusion.1.terms = bf16[8,64,3072]{2,1,0:T(8,128)(2,1)} fusion(bf16[8,96,3072]{2,1,0:T(8,128)(2,1)S(1)} %bitcast.32, f32[8,64]{1,0:T(8,128)S(1)} %copy-done.2), kind=kOutput, calls=%fused_computation.18 | convolution fusion | flops 303611904 | bytes 7866368 | tf_op jit(solution)/shard_map/trj,tjd->trd/dot_general | solution.py:188
  118.5 37.5 %ring_reduce.1 = bf16[64,3072]{1,0:T(8,128)(2,1)} custom-call(bf16[8,64,3072]{2,1,0:T(8,128)(2,1)} %convolution_convert_fusion.1.terms), custom_call_target="tpu_custom_call" | custom-call | tf_op jit(solution)/shard_map/ring_reduce/pallas_call | solution.py:138
  156.0 0.0 copy-done.3
  156.0 1.9 %multiply_convert_fusion = bf16[64,3072]{1,0:T(8,128)(2,1)} fusion(bf16[64,3072]{1,0:T(8,128)(2,1)} %ring_reduce.1, f32[64]{0:T(128)S(1)} %copy-done.3), kind=kLoop, calls=%fused_computation.23 | loop fusion | flops 589824 | bytes 786688 | tf_op jit(solution)/shard_map/convert_element_type | solution.py:190
  (1 shorter events, 0.0 us)
Async XLA Ops:
  45.4 3.4 %copy-start.1 = (f32[8,64]{1,0:T(8,128)}, f32[8,64]{1,0:T(8,128)S(1)}, u32[]{:S(2)}) copy-start(f32[8,64]{1,0:T(8,128)S(1)} %convert_reduce_fusion) | copy-start | bytes 6148
  48.8 11.2 %slice-start = ((s8[12582912]{0:T(1024)(128)(4,1)}), s8[4194304]{0:T(1024)(128)(4,1)S(1)}, s32[]{:S(2)}) async-start(s8[12582912]{0:T(1024)(128)(4,1)} %bitcast.39), calls=%async_computation.2 | async-start | bytes 8388608
  49.2 10.8 %slice-start.1 = ((s8[12582912]{0:T(1024)(128)(4,1)}), s8[4194304]{0:T(1024)(128)(4,1)S(1)}, s32[]{:S(2)}) async-start(s8[12582912]{0:T(1024)(128)(4,1)} %bitcast.39), calls=%async_computation.3 | async-start | bytes 8388608
  57.2 3.9 %slice-start.2 = ((s8[12582912]{0:T(1024)(128)(4,1)}), s8[4194304]{0:T(1024)(128)(4,1)S(1)}, s32[]{:S(2)}) async-start(s8[12582912]{0:T(1024)(128)(4,1)} %bitcast.39), calls=%async_computation.4 | async-start | bytes 8388608
  57.6 2.4 %copy-start = (bf16[8,2,48,3072]{3,2,1,0:T(8,128)(2,1)}, bf16[8,2,48,3072]{3,2,1,0:T(8,128)(2,1)S(1)}, u32[]{:S(2)}) copy-start(bf16[8,2,48,3072]{3,2,1,0:T(8,128)(2,1)S(1)} %copy.11) | copy-start | bytes 14155780
  115.1 0.7 copy-start.2
  115.5 40.4 %copy-start.3 = (f32[64]{0:T(128)S(1)}, f32[64]{0:T(128)}, u32[]{:S(2)}) copy-start(f32[64]{0:T(128)} %param.8) | copy-start | bytes 772

commit v3 on v2

--- a/solution.py
+++ b/solution.py
@@ -168,24 +168,39 @@
         slot_of(expert_ids, experts).astype(jnp.bfloat16)[:, None], (rows, LANES)
     )
     gathered, columns = ring_gather(zigzag, tokens, column)
-    slots = jnp.arange(experts * CAP, dtype=jnp.float32)
-    tables = (columns[:, :, :1].astype(jnp.float32) == slots).astype(jnp.bfloat16)
-
-    outgoing = jnp.einsum("trj,trd->tjd", tables, gathered, preferred_element_type=jnp.float32)
-    outgoing = outgoing.astype(jnp.bfloat16).reshape(size, experts, CAP, width)
-    arrived = lax.all_to_all(
-        outgoing, "expert", split_axis=1, concat_axis=1, tiled=True
-    ).reshape(size * experts * CAP, width)
-    gate_pre = jnp.dot(arrived, gate_weight[0], preferred_element_type=jnp.float32)
-    up_pre = jnp.dot(arrived, up_weight[0], preferred_element_type=jnp.float32)
-    hidden = (jax.nn.gelu(gate_pre, approximate=True) * up_pre).astype(jnp.bfloat16)
-
-    product = jnp.dot(hidden, down_weight[0], preferred_element_type=jnp.float32)
-    product = product.astype(jnp.bfloat16).reshape(size, experts, CAP, width)
-    returned = lax.all_to_all(
-        product, "expert", split_axis=1, concat_axis=1, tiled=True
-    ).reshape(size, experts * CAP, width)
-    placed = jnp.einsum("trj,tjd->trd", tables, returned, preferred_element_type=jnp.float32)
+    here = lax.axis_index("expert")
+    slots = jnp.arange(CAP, dtype=jnp.float32)
+    numbers = columns[:, :, :1].astype(jnp.float32)
+    own_table, away_table = (
+        (numbers == slots + (expert * CAP).astype(jnp.float32)).astype(jnp.bfloat16)
+        for expert in (here, 1 - here)
+    )
+    swap = [(0, 1), (1, 0)]
+
+    def packed(table):
+        rows_of = jnp.einsum("trj,trd->tjd", table, gathered, preferred_element_type=jnp.float32)
+        return rows_of.astype(jnp.bfloat16).reshape(size * CAP, width)
+
+    def hidden_of(arrived):
+        gate_pre = jnp.dot(arrived, gate_weight[0], preferred_element_type=jnp.float32)
+        up_pre = jnp.dot(arrived, up_weight[0], preferred_element_type=jnp.float32)
+        return (jax.nn.gelu(gate_pre, approximate=True) * up_pre).astype(jnp.bfloat16)
+
+    def partial_of(hidden):
+        product = jnp.dot(hidden, down_weight[0], preferred_element_type=jnp.float32)
+        return product.astype(jnp.bfloat16)
+
+    arrived = lax.ppermute(packed(away_table), "expert", swap)
+    own_hidden = hidden_of(packed(own_table))
+    returned = lax.ppermute(partial_of(hidden_of(arrived)), "expert", swap)
+    kept = partial_of(own_hidden)
+    placed = sum(
+        jnp.einsum(
+            "trj,tjd->trd", table, part.reshape(size, CAP, width),
+            preferred_element_type=jnp.float32,
+        )
+        for table, part in ((own_table, kept), (away_table, returned))
+    )
     summed = ring_reduce(zigzag, placed.astype(jnp.bfloat16))
     return (summed.astype(jnp.float32) * gates[:, None]).astype(jnp.bfloat16)
 

time: 158 us -> 159 us (level)
  matrix products: 49.7 us -> 73.7 us
  blocking collectives: 15.4 us -> 0 us
  local copies, waits for them, and re-layouts: 8.51 us -> 0.72 us
    dot_general x4 -> x8, matrix products: 49.7 us -> 73.7 us  [the longest x2 42.9 us: partial_of(): jnp.dot(hidden, down_weight[0], preferred_element_type=jnp.float32)]
    all_to_all x2 -> x0, blocking collectives: 15.4 us -> none  [the longest x1 7.92 us: per_device(): lax.all_to_all(outgoing, 'expert', split_axis=1, concat_axis=1, tiled=True)]
    unnamed x14, local copies, waits for them, and re-layouts: 3.71 us -> 0.04 us
    reshape x2 -> x0, local copies, waits for them, and re-layouts: 3.26 us -> none  [the longest x1 2.83 us: per_device(): product = product.astype(jnp.bfloat16).reshape(size, experts, CAP, width)]
  transfers between devices with their start and end apart: 0 -> 2, of which waited for: 0 -> 0; matrix products, arithmetic and copies ran while one was open for 0% -> 22% of each run, Pallas kernels for 0% -> 0%
where the time goes in v3:
time: 159 us
  Pallas kernels  78.5 us (49%)
  matrix products  73.7 us (46%)
  other arithmetic  5.41 us (3%)
    dot_general x2, matrix products, partial_of(): jnp.dot(hidden, down_weight[0], preferred_element_type=jnp.float32)  42.9 us
    pallas_call x1, Pallas kernels, ring_gather(): pl.pallas_call(functools.partial(gather_kernel, zigzag, size), out_shape=...  41.3 us
    pallas_call x1, Pallas kernels, ring_reduce(): pl.pallas_call(functools.partial(reduce_kernel, zigzag, size), out_shape=...  37.2 us
    dot_general x1, matrix products, hidden_of(): jnp.dot(arrived, gate_weight[0], preferred_element_type=jnp.float32)  10.9 us
    dot_general x1, matrix products, hidden_of(): up_pre = jnp.dot(arrived, up_weight[0], preferred_element_type=jnp.float32)  7.67 us
    dot_general x2, matrix products, per_device(): jnp.einsum('trj,tjd->trd', table, part.reshape(size, CAP, width), preferr...  7.23 us
    dot_general x2, matrix products, packed(): jnp.einsum('trj,trd->tjd', table, gathered, preferred_element_type=jnp.fl...  5.01 us
  transfers between devices with their start and end apart: 2, of which 0 were waited for; matrix products, arithmetic and copies ran while one was open for 22% of the time, Pallas kernels for 0%

profile of v3, /device:TPU:0, one launch (start us, length us, event | category | flops | bytes accessed | tf_op | source)
XLA Modules:
  0.0 159.0 jit_solution(8703758023373179228)
XLA Ops:
  0.0 0.7 fusion.65
  0.7 0.1 reduce_window_sum.11
  0.8 0.8 select_reduce_fusion
  1.7 0.7 fusion.67
  2.3 0.7 broadcast_in_dim.5.column
  3.0 41.3 %ring_gather.1 = (bf16[8,64,3072]{2,1,0:T(8,128)(2,1)}, bf16[8,64,128]{2,1,0:T(8,128)(2,1)}) custom-call(bf16[64,3072]{1,0:T(8,128)(2,1)} %tokens.1, bf16[64,128]{1,0:T(8,128)(2,1)} %broadcast_in_dim.5.column), custom_call_target="tpu_custom_call" | custom-call | tf_op jit(solution)/shard_map/ring_gather/pallas_call | solution.py:120
  44.3 0.0 copy-start
  44.3 1.2 convert_reduce_fusion
  45.5 4.2 %convolution_convert_fusion = bf16[8,48,3072]{2,1,0:T(8,128)(2,1)} fusion(bf16[8,64,3072]{2,1,0:T(8,128)(2,1)} %get-tuple-element.8, f32[8,64]{1,0:T(8,128)S(1)} %convert_reduce_fusion, f32[48]{0:T(128)S(1)} %iota_add_fusion), kind=kOutput, calls=%fused_computation.17 | convolution fusion | flops 152199168 | bytes 5507264 | tf_op jit(solution)/shard_map/trj,trd->tjd/dot_general | solution.py:181
  49.7 0.0 collective-permute-start
  49.7 0.0 copy-done
  49.7 0.0 slice-start
  49.7 0.8 convolution_convert_fusion.1
  50.6 0.0 copy-start.1
  50.6 0.0 slice-start.1
  50.6 0.0 slice-start.2
  50.6 10.9 %fusion.10 = f32[384,2048]{1,0:T(8,128)} fusion(bf16[384,3072]{1,0:T(8,128)(2,1)S(1)} %bitcast.48, bf16[1,3072,2048]{2,1,0:T(8,128)(2,1)} %param.9), kind=kOutput, calls=%fused_computation.10 | convolution fusion | flops 4831838208 | bytes 18087936 | tf_op jit(solution)/shard_map/dot_general | solution.py:185
  61.5 0.0 copy-done.1
  61.6 0.0 collective-permute-done
  61.6 0.0 slice-done
  61.6 0.0 slice-done.1
  61.6 0.0 slice-done.2
  61.6 7.7 %fusion.4 = f32[384,2048]{1,0:T(8,128)} fusion(bf16[384,3072]{1,0:T(8,128)(2,1)} %collective-permute-done, bf16[1,3072,2048]{2,1,0:T(8,128)(2,1)S(1)} %bitcast.54), kind=kOutput, calls=%fused_computation.4 | convolution fusion | flops 4831838208 | bytes 18087936 | tf_op jit(solution)/shard_map/dot_general | solution.py:186
  69.3 0.0 copy-start.2
  69.3 21.8 %fusion.15 = bf16[384,3072]{1,0:T(8,128)(2,1)} fusion(bf16[1,2048,3072]{2,1,0:T(8,128)(2,1)} %param.11, f32[384,2048]{1,0:T(8,128)} %fusion.4, bf16[384,3072]{1,0:T(8,128)(2,1)} %collective-permute-done, bf16[1,3072,2048]{2,1,0:T(8,128)(2,1)} %param.9), kind=kOutput, calls=%fused_computation.16 | convolution fusion | flops 9672720384 | bytes 33030144 | tf_op jit(solution)/shard_map/dot_general | solution.py:190
  91.0 0.5 collective-permute-start.1
  91.5 0.0 copy-done.2
  91.5 21.1 %fusion.12 = bf16[384,3072]{1,0:T(8,128)(2,1)} fusion(bf16[1,2048,3072]{2,1,0:T(8,128)(2,1)} %param.11, f32[384,2048]{1,0:T(8,128)} %fusion.10, bf16[384,3072]{1,0:T(8,128)(2,1)S(1)} %bitcast.49, bf16[1,3072,2048]{2,1,0:T(8,128)(2,1)} %param.10), kind=kOutput, calls=%fused_computation.15 | convolution fusion | flops 9672720384 | bytes 33030144 | tf_op jit(solution)/shard_map/dot_general | solution.py:190
  112.6 2.8 %fusion.54 = f32[8,64,3072]{2,1,0:T(8,128)S(1)} fusion(bf16[8,48,3072]{2,1,0:T(8,128)(2,1)} %bitcast.50, f32[8,64]{1,0:T(8,128)S(1)} %convert_reduce_fusion, f32[48]{0:T(128)S(1)} %iota_add_fusion.1), kind=kOutput, calls=%fused_computation.48 | convolution fusion | flops 151019520 | bytes 8652992 | tf_op jit(solution)/shard_map/trj,tjd->trd/dot_general | solution.py:198
  115.4 0.0 collective-permute-done.1
  115.4 4.5 %add_convert_fusion.terms = bf16[8,64,3072]{2,1,0:T(8,128)(2,1)} fusion(f32[8,64,3072]{2,1,0:T(8,128)S(1)} %fusion.54, bf16[8,48,3072]{2,1,0:T(8,128)(2,1)} %bitcast.9, f32[8,64]{1,0:T(8,128)S(1)} %convert_reduce_fusion, f32[48]{0:T(128)S(1)} %iota_add_fusion), kind=kOutput, calls=%fused_computation.12 | convolution fusion | flops 154165248 | bytes 11798720 | tf_op jit(solution)/shard_map/trj,tjd->trd/dot_general | solution.py:198
  119.9 0.0 copy-start.3
  119.9 37.2 %ring_reduce.1 = bf16[64,3072]{1,0:T(8,128)(2,1)} custom-call(bf16[8,64,3072]{2,1,0:T(8,128)(2,1)} %add_convert_fusion.terms), custom_call_target="tpu_custom_call" | custom-call | tf_op jit(solution)/shard_map/ring_reduce/pallas_call | solution.py:138
  157.1 0.0 copy-done.3
  157.1 1.9 %multiply_convert_fusion = bf16[64,3072]{1,0:T(8,128)(2,1)} fusion(bf16[64,3072]{1,0:T(8,128)(2,1)} %ring_reduce.1, f32[64]{0:T(128)S(1)} %copy-done.3), kind=kLoop, calls=%fused_computation.44 | loop fusion | flops 589824 | bytes 786688 | tf_op jit(solution)/shard_map/convert_element_type | solution.py:205
  (3 shorter events, 0.0 us)
Async XLA Ops:
  44.3 5.4 %copy-start = (bf16[8,64,3072]{2,1,0:T(8,128)(2,1)S(1)}, bf16[8,64,3072]{2,1,0:T(8,128)(2,1)}, u32[]{:S(2)}) copy-start(bf16[8,64,3072]{2,1,0:T(8,128)(2,1)} %get-tuple-element.8) | copy-start | bytes 9437188
  49.7 11.8 %collective-permute-start = (bf16[384,3072]{1,0:T(8,128)(2,1)}, bf16[384,3072]{1,0:T(8,128)(2,1)}, u32[]{:S(2)}, u32[]{:S(2)}) collective-permute-start(bf16[384,3072]{1,0:T(8,128)(2,1)} %bitcast.8), channel_id=1, source_target_pairs={{0,8},{8,0},{1,9},{9,1},{2,10},{10,2},{3,11},{11,3},{4,12},{12,4},... | collective-permute-start | bytes 7077896 | tf_op jit(solution)/shard_map/ppermute | solution.py:193
  49.7 11.8 %slice-start = ((s8[12582912]{0:T(1024)(128)(4,1)}), s8[4194304]{0:T(1024)(128)(4,1)S(1)}, s32[]{:S(2)}) async-start(s8[12582912]{0:T(1024)(128)(4,1)} %bitcast.53), calls=%async_computation | async-start | bytes 8388608
  50.6 11.0 %copy-start.1 = (bf16[8,48,3072]{2,1,0:T(8,128)(2,1)}, bf16[8,48,3072]{2,1,0:T(8,128)(2,1)S(1)}, u32[]{:S(2)}) copy-start(bf16[8,48,3072]{2,1,0:T(8,128)(2,1)S(1)} %convolution_convert_fusion.1) | copy-start | bytes 7077892
  50.6 11.0 %slice-start.1 = ((s8[12582912]{0:T(1024)(128)(4,1)}), s8[4194304]{0:T(1024)(128)(4,1)S(1)}, s32[]{:S(2)}) async-start(s8[12582912]{0:T(1024)(128)(4,1)} %bitcast.53), calls=%async_computation.1 | async-start | bytes 8388608
  50.6 11.0 %slice-start.2 = ((s8[12582912]{0:T(1024)(128)(4,1)}), s8[4194304]{0:T(1024)(128)(4,1)S(1)}, s32[]{:S(2)}) async-start(s8[12582912]{0:T(1024)(128)(4,1)} %bitcast.53), calls=%async_computation.2 | async-start | bytes 8388608
  69.3 22.3 %copy-start.2 = (bf16[8,48,3072]{2,1,0:T(8,128)(2,1)S(1)}, bf16[8,48,3072]{2,1,0:T(8,128)(2,1)}, u32[]{:S(2)}) copy-start(bf16[8,48,3072]{2,1,0:T(8,128)(2,1)} %copy-done.1) | copy-start | bytes 7077892
  91.0 24.4 %collective-permute-start.1 = (bf16[384,3072]{1,0:T(8,128)(2,1)}, bf16[384,3072]{1,0:T(8,128)(2,1)}, u32[]{:S(2)}, u32[]{:S(2)}) collective-permute-start(bf16[384,3072]{1,0:T(8,128)(2,1)} %fusion.15), channel_id=1, source_target_pairs={{0,8},{8,0},{1,9},{9,1},{2,10},{10,2},{3,11},{11,3},{4,12},{12,4},... | collective-permute-start | bytes 7077896 | tf_op jit(solution)/shard_map/ppermute | solution.py:195
  119.9 37.2 %copy-start.3 = (f32[64]{0:T(128)S(1)}, f32[64]{0:T(128)}, u32[]{:S(2)}) copy-start(f32[64]{0:T(128)} %param.8) | copy-start | bytes 772
